TPU v7x, 32 devices: a whole 2x2x4 slice. The times are simulated.
32 devices in a mesh: groups: 2 (over y), feat: 4 (over z), layer: 2 (over x), row: 2 (over core).
Axes of the slice: x: 2, y: 2, z: 4, core: 2. Of those that a mesh axis runs over, the one named last changes fastest.
Arguments:
- resid_buf: bfloat16 [512, 2, 4608], P(('groups', 'feat', 'row')), parts along dimension 0, may hold values from -6 to 6
- shuffle: int32 [512], P('groups'), parts along dimension 0, may hold values from 0 to 255, each once
- mlp_out: bfloat16 [512, 2, 4608], P(('groups', 'feat', 'row')), parts along dimension 0, may hold values from -5 to 5
- enc_weight: bfloat16 [2, 8192, 4608], P('layer', 'feat', 'row'), may hold values from -0.09375 to 0.09375
- dec_weight: bfloat16 [2, 8192, 2, 4608], P('layer', 'feat', None, 'row'), may hold values from -0.0625 to 0.0625
- enc_bias: float32 [2, 8192], P('layer', 'feat'), may hold values from -0.5 to 0.5
- dec_bias: float32 [2, 4608], replicated, may hold values from -3 to 3
Outputs:
- rebuilt: bfloat16 [512, 2, 4608], P(('groups', 'feat', 'row')), parts along dimension 0
- enc_grad: bfloat16 [4, 8192, 4608], P(('groups', 'layer'), 'feat', 'row'), parts along dimension 0
- dec_grad: bfloat16 [4, 8192, 2, 4608], P(('groups', 'layer'), 'feat', None, 'row'), parts along dimension 0
- bias_grad: float32 [4, 8192], P(('groups', 'layer'), 'feat'), parts along dimension 0
There are 2 independent parts, one for each index of `groups`. A program takes and returns all parts, laid end to end along the dimension named above; an argument that names none is the same for every part. Nothing has to cross between parts.
Inputs may be any that keep to these rules, and one draw needn't show every extreme that they name: `shuffle`: a permutation of the 256 buffer rows.
All inputs are finite; a program needn't handle non-finite values.
Results may differ from a plain program's by a relative error of at most 0.04.
Values may be sent and summed in bfloat16 or wider, within the bound.
A program may use at most 128 MiB of HBM per device.

v0:
```python
import jax
import jax.numpy as jnp
from jax import lax
from jax.sharding import PartitionSpec as P

LAYERS = 2


def from_behind(block, axis, distance):
    devices = range(lax.axis_size(axis))
    route = [(i - distance, i) for i in devices if i - distance in devices]
    return lax.ppermute(block, axis, route)


def dot_last(left, right):
    return lax.dot_general(
        left, right, (((1,), (1,)), ((), ())), preferred_element_type=jnp.float32
    )


def dot_first(left, right):
    return lax.dot_general(
        left, right, (((0,), (0,)), ((), ())), preferred_element_type=jnp.float32
    )


def on_device(resid_buf, shuffle, mlp_out, enc_weight, dec_weight, enc_bias, dec_bias):
    feat_count = lax.axis_size("feat")
    row_count = lax.axis_size("row")
    sub_blocks = lax.axis_size("layer") // LAYERS
    layer_pos = lax.axis_index("layer")
    row_pos = lax.axis_index("row")
    source = layer_pos // sub_blocks
    rows_each = resid_buf.shape[0]
    width = dec_bias.shape[1]
    half_width = enc_weight.shape[2]
    local_rows = rows_each * feat_count
    total_rows = local_rows * row_count
    loss_scale = float(total_rows) ** (-0.5)
    own_layer = lax.dynamic_index_in_dim(resid_buf, source, axis=1, keepdims=False)
    buffer_all = lax.all_gather(own_layer, ("feat", "row"), axis=0, tiled=True)
    batch_rows = jnp.take(buffer_all, shuffle, axis=0)
    blocks = batch_rows.reshape(feat_count, row_count, rows_each, width)
    inputs_half = lax.dynamic_slice_in_dim(
        jnp.swapaxes(blocks, 0, 1), row_pos * half_width, half_width, axis=3
    )
    inputs_half = inputs_half.reshape(total_rows, half_width)
    own_half_dec = dec_weight[0][:, 0]
    next_half_dec = dec_weight[0][:, 1]
    pre_all = lax.psum(dot_last(inputs_half, enc_weight[0]), "row") + enc_bias[0]
    features_all = jnp.maximum(pre_all, 0.0).astype(jnp.bfloat16)
    own_part = jnp.dot(features_all, own_half_dec, preferred_element_type=jnp.float32)
    next_part = jnp.dot(features_all, next_half_dec, preferred_element_type=jnp.float32)
    carried = from_behind(next_part, "layer", sub_blocks)
    spread = (own_part + carried).reshape(row_count, local_rows, half_width)
    halves = lax.psum_scatter(spread, "feat", scatter_dimension=1, tiled=True)
    joined = lax.all_to_all(halves, "row", split_axis=0, concat_axis=2, tiled=True)
    section_sum = joined.reshape(rows_each, width)
    target_ids = jnp.arange(LAYERS, dtype=jnp.int32)
    target_slots = jnp.where((target_ids == source)[:, None, None], section_sum[None], 0.0)
    totals = lax.psum(target_slots, "layer")
    recon_sum = jnp.swapaxes(totals, 0, 1) + dec_bias[None]
    errors = (recon_sum - mlp_out.astype(jnp.float32)).astype(jnp.bfloat16)
    gathered = lax.all_gather(errors, ("feat", "row"), axis=0, tiled=True)
    error_grid = gathered.reshape(feat_count, row_count, rows_each, LAYERS, width)
    errors_mine = lax.dynamic_index_in_dim(error_grid, row_pos, axis=1, keepdims=False)
    errors_mine = errors_mine.reshape(local_rows, LAYERS, width)
    errors_half = lax.dynamic_slice_in_dim(
        jnp.swapaxes(error_grid, 0, 1), row_pos * half_width, half_width, axis=4
    )
    errors_half = errors_half.reshape(total_rows, LAYERS, half_width)
    live_next = source + 1 < LAYERS
    next_index = jnp.minimum(source + 1, LAYERS - 1)
    half_own = lax.dynamic_index_in_dim(errors_half, source, axis=1, keepdims=False)
    half_next = lax.dynamic_index_in_dim(errors_half, next_index, axis=1, keepdims=False)
    half_next = jnp.where(live_next, half_next, jnp.zeros_like(half_next))
    half_terms = dot_last(half_own, own_half_dec) + dot_last(half_next, next_half_dec)
    grad_feats = lax.psum(half_terms, "row") * loss_scale
    grad_all = jnp.where(pre_all > 0, grad_feats, 0.0).astype(jnp.bfloat16)
    grad_own = loss_scale * dot_first(features_all, half_own)
    grad_next = loss_scale * dot_first(features_all, half_next)
    enc_grad = dot_first(grad_all, inputs_half).astype(jnp.bfloat16)
    dec_grad = jnp.stack([grad_own, grad_next], axis=1).astype(jnp.bfloat16)
    bias_grad = jnp.sum(grad_all.astype(jnp.float32), axis=0)
    return (recon_sum.astype(jnp.bfloat16), enc_grad[None], dec_grad[None], bias_grad[None])


def solution(mesh):
    return jax.shard_map(
        on_device,
        mesh=mesh,
        in_specs=(
            P(("groups", "feat", "row"), None, None),
            P("groups"),
            P(("groups", "feat", "row"), None, None),
            P("layer", "feat", "row"),
            P("layer", "feat", None, "row"),
            P("layer", "feat"),
            P(),
        ),
        out_specs=(
            P(("groups", "feat", "row"), None, None),
            P(("groups", "layer"), "feat", "row"),
            P(("groups", "layer"), "feat", None, "row"),
            P(("groups", "layer"), "feat"),
        ),
        check_vma=False,
    )
```

profile of v0, /device:TPU:0, one launch (start us, length us, event | category | flops | bytes accessed | tf_op | source)
XLA Modules:
  0.0 529.7 jit_solution(15762774988231695739)
XLA Ops:
  9.8 34.6 %all-gather.6.cloned.1.call-done = bf16[256,1,4608]{2,0,1:T(8,128)(2,1)} async-done(((bf16[32,1,4608]{2,0,1:T(8,128)(2,1)}), bf16[256,1,4608]{2,0,1:T(8,128)(2,1)}) %all-gather.6.cloned.1.call-update) | async-done | bytes 2359312 | tf_op jit(solution)/shard_map/all_gather | solution.py:41
  44.4 6.3 %gather_fusion = bf16[256,4608]{1,0:T(8,128)(2,1)S(1)} fusion(bf16[256,4608]{1,0:T(8,128)(2,1)} %bitcast.65, s32[1024]{0:T(1024)S(1)} %pad_clamp_fusion), kind=kCustom, calls=%fused_computation | custom fusion | bytes 4719616 | tf_op jit(solution)/shard_map/jit(_take)/gather | solution.py:42
  52.0 7.6 %fusion.3 = f32[256,2048]{1,0:T(8,128)} fusion(bf16[256,2304]{1,0:T(8,128)(2,1)S(1)} %bitcast.71, bf16[1,2048,2304]{2,1,0:T(8,128)(2,1)} %param.10), kind=kOutput, calls=%fused_computation.11 | convolution fusion | flops 2415919104 | bytes 12713984 | tf_op jit(solution)/shard_map/dot_general | solution.py:16
  59.7 18.2 %copy.45 = bf16[1,2048,2,2304]{3,1,2,0:T(8,128)(2,1)} copy(bf16[1,2048,2,2304]{3,2,1,0:T(2,128)(2,1)} %param.11) | data formatting | bytes 37748736 | tf_op args[4]
  77.9 2.4 all-reduce.6.cloned.1.call-done
  80.4 2.0 maximum_convert_fusion
  82.3 6.6 %fusion.8 = f32[256,2304]{1,0:T(8,128)S(1)} fusion(bf16[256,2048]{1,0:T(8,128)(2,1)S(1)} %maximum_convert_fusion, bf16[2048,2,2304]{2,0,1:T(8,128)(2,1)} %bitcast.66), kind=kOutput, calls=%fused_computation.16 | convolution fusion | flops 2415919104 | bytes 12845056 | tf_op jit(solution)/shard_map/dot_general | solution.py:53
  89.0 4.1 collective-permute-start
  93.1 50.6 %collective-permute-done = f32[256,2304]{1,0:T(8,128)S(1)} collective-permute-done((f32[256,2304]{1,0:T(8,128)S(1)}, f32[256,2304]{1,0:T(8,128)S(1)}, u32[]{:S(2)}, u32[]{:S(2)}) %collective-permute-start) | collective-permute-done | bytes 2359328 | tf_op jit(solution)/shard_map/ppermute | solution.py:12
  143.7 2.7 fusion.9
  146.4 3.2 copy.32
  151.5 94.8 %all-reduce.12.cloned.1.call-done = f32[2,128,2304]{2,0,1:T(2,128)} async-done(((f32[2,128,2304]{2,0,1:T(2,128)}), f32[2,128,2304]{2,0,1:T(2,128)}) %all-reduce.12.cloned.1.call-update) | async-done | bytes 2359312
  247.5 4.2 all_to_all.15
  253.5 42.1 %all-reduce.8.cloned.1.call-done = f32[2,32,4608]{2,1,0:T(8,128)} async-done(((f32[2,32,4608]{2,1,0:T(8,128)}), f32[2,32,4608]{2,1,0:T(8,128)}) %all-reduce.8.cloned.1.call-update) | async-done | bytes 1179664 | tf_op jit(solution)/shard_map/psum | solution.py:61
  295.6 2.5 fusion.15
  299.7 49.8 %all-gather.4.cloned.1.call-done = bf16[256,2,4608]{2,0,1:T(8,128)(2,1)} async-done(((bf16[32,2,4608]{2,0,1:T(8,128)(2,1)}), bf16[256,2,4608]{2,0,1:T(8,128)(2,1)}) %all-gather.4.cloned.1.call-update) | async-done | bytes 4718608 | tf_op jit(solution)/shard_map/all_gather | solution.py:64
  351.5 6.1 %fusion.5 = f32[256,2048]{1,0:T(8,128)S(1)} fusion(bf16[2048,2,2304]{2,0,1:T(8,128)(2,1)} %bitcast.67, bf16[256,2,2304]{2,0,1:T(8,128)(2,1)S(1)} %bitcast.73, s32[]{:T(128)S(6)} %select_n.47), kind=kOutput, calls=%fused_computation.13 | convolution fusion | flops 2415919104 | bytes 12713988 | tf_op jit(solution)/shard_map/dot_general | solution.py:16
  357.6 7.7 %fusion.10 = f32[256,2048]{1,0:T(8,128)} fusion(f32[256,2048]{1,0:T(8,128)S(1)} %fusion.5, bf16[2048,2,2304]{2,0,1:T(8,128)(2,1)} %bitcast.68, bf16[256,2,2304]{2,0,1:T(8,128)(2,1)S(1)} %bitcast.74, s32[]{:T(128)S(6)} %select_n.52, pred[]{:T(512)S(6)} %lt.28), kind=kOutput, calls=%fused_computation.18 | convolution fusion | flops 2417033216 | bytes 14811141 | tf_op jit(solution)/shard_map/dot_general | solution.py:16
  365.3 4.4 fusion.1
  369.7 5.2 fusion.2
  374.9 7.4 %pad_maximum_fusion = bf16[1,2048,2,2304]{3,1,2,0:T(8,128)(2,1)S(1)} fusion(bf16[1,2048,1,2304]{3,1,2,0:T(8,128)(2,1)} %fusion.2, bf16[1,2048,1,2304]{3,1,2,0:T(8,128)(2,1)S(1)} %fusion.1), kind=kLoop, calls=%fused_computation.1 | loop fusion | flops 9437184 | bytes 37748736 | tf_op jit(solution)/shard_map/stack | solution.py:83
  382.3 132.7 %copy.38 = bf16[1,2048,2,2304]{3,2,1,0:T(2,128)(2,1)} copy(bf16[1,2048,2,2304]{3,1,2,0:T(8,128)(2,1)S(1)} %pad_maximum_fusion) | data formatting | bytes 37748736
  515.0 2.7 convert_reduce_fusion
  517.7 5.2 fusion
  (58 shorter events, 11.7 us)
Async XLA Ops:
  7.2 1.1 copy-start
  7.2 2.5 copy-start.11
  7.2 37.2 %all-gather.6.cloned.1.call-start = ((), (), s32[]{:S(2)}) async-start(), calls=%async_computation.5 | async-start | bytes 2654208 | tf_op jit(solution)/shard_map/all_gather | solution.py:41
  9.6 70.7 %all-reduce.6.cloned.1.call-start = ((), (), s32[]{:S(2)}) async-start(), calls=%async_computation.1 | async-start | bytes 4194304 | tf_op jit(solution)/shard_map/psum | solution.py:50
  51.0 1.0 copy-start.4
  59.7 20.7 %copy-start.10 = (f32[1,2048]{1,0:T(1,128)S(1)}, f32[1,2048]{1,0:T(1,128)}, u32[]{:S(2)}) copy-start(f32[1,2048]{1,0:T(1,128)} %param.12) | copy-start | bytes 24580
  59.7 186.7 %all-reduce.12.cloned.1.call-start = ((), (), s32[]{:S(2)}) async-start(), calls=%async_computation.6 | async-start | bytes 4718592
  80.4 63.3 %copy-start.2 = (bf16[1,2048,2,2304]{3,1,2,0:T(8,128)(2,1)S(1)}, bf16[1,2048,2,2304]{3,1,2,0:T(8,128)(2,1)}, u32[]{:S(2)}) copy-start(bf16[1,2048,2,2304]{3,1,2,0:T(8,128)(2,1)} %copy.45) | copy-start | bytes 56623108
  89.0 54.7 %collective-permute-start = (f32[256,2304]{1,0:T(8,128)S(1)}, f32[256,2304]{1,0:T(8,128)S(1)}, u32[]{:S(2)}, u32[]{:S(2)}) collective-permute-start(f32[256,2304]{1,0:T(8,128)S(1)} %fusion.8), channel_id=1, source_target_pairs={{0,2},{1,3},{4,6},{5,7},{8,10},{9,11},{12,14},{13,15},{16,18},{17,... | collective-permute-start | bytes 7077896 | tf_op jit(solution)/shard_map/ppermute | solution.py:12
  149.6 0.7 copy-start.12
  149.7 145.9 %all-reduce.8.cloned.1.call-start = ((), (), s32[]{:S(2)}) async-start(), calls=%async_computation.2 | async-start | bytes 2359296 | tf_op jit(solution)/shard_map/psum | solution.py:61
  252.2 43.4 %copy-start.9 = (f32[2,4608]{1,0:T(2,128)S(1)}, f32[2,4608]{1,0:T(2,128)}, u32[]{:S(2)}) copy-start(f32[2,4608]{1,0:T(2,128)} %param.13) | copy-start | bytes 110596
  253.4 96.0 %all-gather.4.cloned.1.call-start = ((), (), s32[]{:S(2)}) async-start(), calls=%async_computation.3 | async-start | bytes 5308416 | tf_op jit(solution)/shard_map/all_gather | solution.py:64
  295.6 2.6 copy-start.6
  298.1 216.9 %all-reduce.10.cloned.1.call-start = ((), (), s32[]{:S(2)}) async-start(), calls=%async_computation.4 | async-start | bytes 4194304 | tf_op jit(solution)/shard_map/psum | solution.py:78
  351.5 6.1 %copy-start.7 = (bf16[2,4,32,2,2304]{4,2,1,0,3:T(8,128)(2,1)}, bf16[2,4,32,2,2304]{4,2,1,0,3:T(8,128)(2,1)S(1)}, u32[]{:S(2)}) copy-start(bf16[2,4,32,2,2304]{4,2,1,0,3:T(8,128)(2,1)S(1)} %copy.36) | copy-start | bytes 7077892
  365.3 4.4 copy-start.8
  382.3 132.7 %copy-start.3 = (f32[256,2048]{1,0:T(8,128)S(1)}, f32[256,2048]{1,0:T(8,128)}, u32[]{:S(2)}) copy-start(f32[256,2048]{1,0:T(8,128)} %all-reduce.6.cloned.1.call-done) | copy-start | bytes 6291460
  515.0 2.7 copy-start.5
  517.7 5.2 copy-start.1
Sparse Core Ops, SparseCore 0:
  10.2 34.1 all-gather.5
  59.8 20.5 all-reduce.5
  149.8 96.5 all-reduce.11
  253.6 41.9 all-reduce.7
  298.2 51.1 all-gather.3
  365.4 20.0 all-reduce.9
where the time goes:
time: 530 us
  waiting for transfers between devices  274 us (52%)
  local copies, waits for them, and re-layouts  170 us (32%)
  matrix products  45.5 us (9%)
  other arithmetic  16.1 us (3%)
  between operations  15 us (3%)
    unnamed x33, local copies, waits for them, and re-layouts  157 us
    unnamed x7, waiting for transfers between devices  94.9 us
    ppermute x1, waiting for transfers between devices, from_behind(): return lax.ppermute(block, axis, route)  50.6 us
    all_gather x1, waiting for transfers between devices, on_device(): gathered = lax.all_gather(errors, ('feat', 'row'), axis=0, tiled=True)  49.8 us
    psum x1, waiting for transfers between devices, on_device(): totals = lax.psum(target_slots, 'layer')  42.1 us
    all_gather x1, waiting for transfers between devices, on_device(): buffer_all = lax.all_gather(own_layer, ('feat', 'row'), axis=0, tiled=True)  34.6 us
    dot_general x3, matrix products, dot_last(): lax.dot_general(left, right, (((1,), (1,)), ((), ())), preferred_element_...  21.3 us
    dot_general x3, matrix products, dot_first(): lax.dot_general(left, right, (((0,), (0,)), ((), ())), preferred_element_...  14.8 us
  transfers between devices with their start and end apart: 7, of which 6 were waited for; matrix products, arithmetic and copies ran while one was open for 32% of the time, Pallas kernels for 0%

commit v1 on v0

--- a/solution.py
+++ b/solution.py
@@ -1,9 +1,18 @@
+import functools
 import jax
 import jax.numpy as jnp
 from jax import lax
 from jax.sharding import PartitionSpec as P
 
 LAYERS = 2
+
+
+def knots_prepare(xin, group_axis):
+    upper = lax.all_gather(xin, axis_name=group_axis).sum(axis=0)
+    return upper
+
+
+_number_thing = functools.partial(knots_prepare, group_axis="layer")
 
 
 def from_behind(block, axis, distance):
@@ -58,7 +67,7 @@
     section_sum = joined.reshape(rows_each, width)
     target_ids = jnp.arange(LAYERS, dtype=jnp.int32)
     target_slots = jnp.where((target_ids == source)[:, None, None], section_sum[None], 0.0)
-    totals = lax.psum(target_slots, "layer")
+    totals = _number_thing(target_slots)
     recon_sum = jnp.swapaxes(totals, 0, 1) + dec_bias[None]
     errors = (recon_sum - mlp_out.astype(jnp.float32)).astype(jnp.bfloat16)
     gathered = lax.all_gather(errors, ("feat", "row"), axis=0, tiled=True)

time: 530 us -> 524 us (0.989)
  waiting for transfers between devices: 274 us -> 268 us
    psum x1 -> x0, waiting for transfers between devices: 42.1 us -> none  [on_device(): totals = lax.psum(target_slots, 'layer')]
    all_gather x0 -> x1, waiting for transfers between devices: none -> 35.2 us  [knots_prepare(): upper = lax.all_gather(xin, axis_name=group_axis).sum(axis=0)]
  transfers between devices with their start and end apart: 7 -> 7, of which waited for: 6 -> 6; matrix products, arithmetic and copies ran while one was open for 32% -> 33% of each run, Pallas kernels for 0% -> 0%
where the time goes in v1:
time: 524 us; the launch traced here: 523 us
  waiting for transfers between devices  268 us (51%)
  local copies, waits for them, and re-layouts  170 us (32%)
  matrix products  45.4 us (9%)
  other arithmetic  16.5 us (3%)
  between operations  15 us (3%)
    unnamed x33, local copies, waits for them, and re-layouts  157 us
    unnamed x7, waiting for transfers between devices  94.9 us
    ppermute x1, waiting for transfers between devices, from_behind(): return lax.ppermute(block, axis, route)  50.6 us
    all_gather x1, waiting for transfers between devices, on_device(): gathered = lax.all_gather(errors, ('feat', 'row'), axis=0, tiled=True)  49.8 us
    all_gather x1, waiting for transfers between devices, knots_prepare(): upper = lax.all_gather(xin, axis_name=group_axis).sum(axis=0)  35.2 us
    all_gather x1, waiting for transfers between devices, on_device(): buffer_all = lax.all_gather(own_layer, ('feat', 'row'), axis=0, tiled=True)  34.6 us
    dot_general x3, matrix products, dot_last(): lax.dot_general(left, right, (((1,), (1,)), ((), ())), preferred_element_...  21.3 us
    dot_general x3, matrix products, dot_first(): lax.dot_general(left, right, (((0,), (0,)), ((), ())), preferred_element_...  14.8 us
  transfers between devices with their start and end apart: 7, of which 6 were waited for; matrix products, arithmetic and copies ran while one was open for 33% of the time, Pallas kernels for 0%

profile of v1, /device:TPU:0, one launch (start us, length us, event | category | flops | bytes accessed | tf_op | source)
XLA Modules:
  0.0 523.2 jit_solution(17151724039423448602)
XLA Ops:
  9.8 34.6 %all-gather.9.cloned.1.call-done = bf16[256,1,4608]{2,0,1:T(8,128)(2,1)} async-done(((bf16[32,1,4608]{2,0,1:T(8,128)(2,1)}), bf16[256,1,4608]{2,0,1:T(8,128)(2,1)}) %all-gather.9.cloned.1.call-update) | async-done | bytes 2359312 | tf_op jit(solution)/shard_map/all_gather | solution.py:50
  44.4 6.3 %gather_fusion = bf16[256,4608]{1,0:T(8,128)(2,1)S(1)} fusion(bf16[256,4608]{1,0:T(8,128)(2,1)} %bitcast.65, s32[1024]{0:T(1024)S(1)} %pad_clamp_fusion), kind=kCustom, calls=%fused_computation | custom fusion | bytes 4719616 | tf_op jit(solution)/shard_map/jit(_take)/gather | solution.py:51
  52.0 7.6 %fusion.3 = f32[256,2048]{1,0:T(8,128)} fusion(bf16[256,2304]{1,0:T(8,128)(2,1)S(1)} %bitcast.71, bf16[1,2048,2304]{2,1,0:T(8,128)(2,1)} %param.10), kind=kOutput, calls=%fused_computation.11 | convolution fusion | flops 2415919104 | bytes 12713984 | tf_op jit(solution)/shard_map/dot_general | solution.py:25
  59.7 18.2 %copy.45 = bf16[1,2048,2,2304]{3,1,2,0:T(8,128)(2,1)} copy(bf16[1,2048,2,2304]{3,2,1,0:T(2,128)(2,1)} %param.11) | data formatting | bytes 37748736 | tf_op args[4]
  77.9 2.4 all-reduce.5.cloned.1.call-done
  80.4 2.0 maximum_convert_fusion
  82.3 6.6 %fusion.8 = f32[256,2304]{1,0:T(8,128)S(1)} fusion(bf16[256,2048]{1,0:T(8,128)(2,1)S(1)} %maximum_convert_fusion, bf16[2048,2,2304]{2,0,1:T(8,128)(2,1)} %bitcast.66), kind=kOutput, calls=%fused_computation.16 | convolution fusion | flops 2415919104 | bytes 12845056 | tf_op jit(solution)/shard_map/dot_general | solution.py:62
  89.0 4.1 collective-permute-start
  93.1 50.6 %collective-permute-done = f32[256,2304]{1,0:T(8,128)S(1)} collective-permute-done((f32[256,2304]{1,0:T(8,128)S(1)}, f32[256,2304]{1,0:T(8,128)S(1)}, u32[]{:S(2)}, u32[]{:S(2)}) %collective-permute-start) | collective-permute-done | bytes 2359328 | tf_op jit(solution)/shard_map/ppermute | solution.py:21
  143.7 2.7 fusion.9
  146.4 3.2 copy.32
  151.5 94.8 %all-reduce.9.cloned.1.call-done = f32[2,128,2304]{2,0,1:T(2,128)} async-done(((f32[2,128,2304]{2,0,1:T(2,128)}), f32[2,128,2304]{2,0,1:T(2,128)}) %all-reduce.9.cloned.1.call-update) | async-done | bytes 2359312
  247.5 4.2 all_to_all.15
  253.5 35.2 %all-gather.5.cloned.1.call-done = f32[2,2,32,4608]{3,2,1,0:T(8,128)} async-done(((f32[1,2,32,4608]{3,2,1,0:T(8,128)}), f32[2,2,32,4608]{3,2,1,0:T(8,128)}) %all-gather.5.cloned.1.call-update) | async-done | bytes 2359312 | tf_op jit(solution)/shard_map/all_gather | solution.py:11
  288.7 1.9 reduce_sum.18
  293.2 49.8 %all-gather.7.cloned.1.call-done = bf16[256,2,4608]{2,0,1:T(8,128)(2,1)} async-done(((bf16[32,2,4608]{2,0,1:T(8,128)(2,1)}), bf16[256,2,4608]{2,0,1:T(8,128)(2,1)}) %all-gather.7.cloned.1.call-update) | async-done | bytes 4718608 | tf_op jit(solution)/shard_map/all_gather | solution.py:73
  345.0 6.0 %fusion.5 = f32[256,2048]{1,0:T(8,128)S(1)} fusion(bf16[2048,2,2304]{2,0,1:T(8,128)(2,1)} %bitcast.67, bf16[256,2,2304]{2,0,1:T(8,128)(2,1)S(1)} %bitcast.73, s32[]{:T(128)S(6)} %select_n.54), kind=kOutput, calls=%fused_computation.13 | convolution fusion | flops 2415919104 | bytes 12713988 | tf_op jit(solution)/shard_map/dot_general | solution.py:25
  351.1 7.7 %fusion.10 = f32[256,2048]{1,0:T(8,128)} fusion(f32[256,2048]{1,0:T(8,128)S(1)} %fusion.5, bf16[2048,2,2304]{2,0,1:T(8,128)(2,1)} %bitcast.68, bf16[256,2,2304]{2,0,1:T(8,128)(2,1)S(1)} %bitcast.74, s32[]{:T(128)S(6)} %select_n.59, pred[]{:T(512)S(6)} %lt.28), kind=kOutput, calls=%fused_computation.18 | convolution fusion | flops 2417033216 | bytes 14811141 | tf_op jit(solution)/shard_map/dot_general | solution.py:25
  358.8 4.4 fusion.1
  363.2 5.2 fusion.2
  368.4 7.4 %pad_maximum_fusion = bf16[1,2048,2,2304]{3,1,2,0:T(8,128)(2,1)S(1)} fusion(bf16[1,2048,1,2304]{3,1,2,0:T(8,128)(2,1)} %fusion.2, bf16[1,2048,1,2304]{3,1,2,0:T(8,128)(2,1)S(1)} %fusion.1), kind=kLoop, calls=%fused_computation.1 | loop fusion | flops 9437184 | bytes 37748736 | tf_op jit(solution)/shard_map/stack | solution.py:92
  375.8 132.7 %copy.38 = bf16[1,2048,2,2304]{3,2,1,0:T(2,128)(2,1)} copy(bf16[1,2048,2,2304]{3,1,2,0:T(8,128)(2,1)S(1)} %pad_maximum_fusion) | data formatting | bytes 37748736
  508.5 2.7 convert_reduce_fusion
  511.2 5.2 fusion
  (59 shorter events, 12.6 us)
Async XLA Ops:
  7.2 1.1 copy-start
  7.2 2.5 copy-start.11
  7.2 37.2 %all-gather.9.cloned.1.call-start = ((), (), s32[]{:S(2)}) async-start(), calls=%async_computation.5 | async-start | bytes 2654208 | tf_op jit(solution)/shard_map/all_gather | solution.py:50
  9.6 70.7 %all-reduce.5.cloned.1.call-start = ((), (), s32[]{:S(2)}) async-start(), calls=%async_computation.1 | async-start | bytes 4194304 | tf_op jit(solution)/shard_map/psum | solution.py:59
  51.0 1.0 copy-start.4
  59.7 20.7 %copy-start.10 = (f32[1,2048]{1,0:T(1,128)S(1)}, f32[1,2048]{1,0:T(1,128)}, u32[]{:S(2)}) copy-start(f32[1,2048]{1,0:T(1,128)} %param.12) | copy-start | bytes 24580
  59.7 186.7 %all-reduce.9.cloned.1.call-start = ((), (), s32[]{:S(2)}) async-start(), calls=%async_computation.6 | async-start | bytes 4718592
  80.4 63.3 %copy-start.2 = (bf16[1,2048,2,2304]{3,1,2,0:T(8,128)(2,1)S(1)}, bf16[1,2048,2,2304]{3,1,2,0:T(8,128)(2,1)}, u32[]{:S(2)}) copy-start(bf16[1,2048,2,2304]{3,1,2,0:T(8,128)(2,1)} %copy.45) | copy-start | bytes 56623108
  89.0 54.7 %collective-permute-start = (f32[256,2304]{1,0:T(8,128)S(1)}, f32[256,2304]{1,0:T(8,128)S(1)}, u32[]{:S(2)}, u32[]{:S(2)}) collective-permute-start(f32[256,2304]{1,0:T(8,128)S(1)} %fusion.8), channel_id=1, source_target_pairs={{0,2},{1,3},{4,6},{5,7},{8,10},{9,11},{12,14},{13,15},{16,18},{17,... | collective-permute-start | bytes 7077896 | tf_op jit(solution)/shard_map/ppermute | solution.py:21
  149.6 0.7 copy-start.12
  149.7 139.0 %all-gather.5.cloned.1.call-start = ((), (), s32[]{:S(2)}) async-start(), calls=%async_computation.2 | async-start | bytes 3538944 | tf_op jit(solution)/shard_map/all_gather | solution.py:11
  253.4 37.2 %copy-start.8 = (bf16[32,2,4608]{2,1,0:T(2,128)(2,1)S(1)}, bf16[32,2,4608]{2,1,0:T(2,128)(2,1)}, u32[]{:S(2)}) copy-start(bf16[32,2,4608]{2,1,0:T(2,128)(2,1)} %param.9) | copy-start | bytes 1769476
  253.4 37.2 %copy-start.9 = (f32[2,4608]{1,0:T(2,128)S(1)}, f32[2,4608]{1,0:T(2,128)}, u32[]{:S(2)}) copy-start(f32[2,4608]{1,0:T(2,128)} %param.13) | copy-start | bytes 110596
  253.4 89.5 %all-gather.7.cloned.1.call-start = ((), (), s32[]{:S(2)}) async-start(), calls=%async_computation.3 | async-start | bytes 5308416 | tf_op jit(solution)/shard_map/all_gather | solution.py:73
  291.6 216.9 %all-reduce.7.cloned.1.call-start = ((), (), s32[]{:S(2)}) async-start(), calls=%async_computation.4 | async-start | bytes 4194304 | tf_op jit(solution)/shard_map/psum | solution.py:87
  345.0 6.1 %copy-start.6 = (bf16[2,4,32,2,2304]{4,2,1,0,3:T(8,128)(2,1)}, bf16[2,4,32,2,2304]{4,2,1,0,3:T(8,128)(2,1)S(1)}, u32[]{:S(2)}) copy-start(bf16[2,4,32,2,2304]{4,2,1,0,3:T(8,128)(2,1)S(1)} %copy.36) | copy-start | bytes 7077892
  358.8 4.4 copy-start.7
  375.8 132.7 %copy-start.3 = (f32[256,2048]{1,0:T(8,128)S(1)}, f32[256,2048]{1,0:T(8,128)}, u32[]{:S(2)}) copy-start(f32[256,2048]{1,0:T(8,128)} %all-reduce.5.cloned.1.call-done) | copy-start | bytes 6291460
  508.5 2.7 copy-start.5
  511.2 5.2 copy-start.1
Sparse Core Ops, SparseCore 0:
  10.2 34.1 all-gather.8
  59.8 20.5 all-reduce.4
  149.8 96.5 all-reduce.8
  253.6 35.0 all-gather.4
  291.7 51.1 all-gather.6
  358.9 20.0 all-reduce.6
